TPU v7x, 256 devices: a whole 4x4x8 slice. The times are simulated.
256 devices in a mesh: seq: 32 (over y_hi, z, core), head: 8 (over y_lo, x).
Axes of the slice: x: 4, y: 4 (y_hi: 2, y_lo: 2; y = y_hi * 2 + y_lo), z: 8, core: 2. Of those that a mesh axis runs over, the one named last changes fastest.
Arguments:
- q_cells: bfloat16 [8192, 8192], P('seq', 'head'), may hold values from -60 to 60
- k_cells: bfloat16 [8192, 1024], P('seq', 'head'), may hold values from -11 to 11
- v_cells: bfloat16 [8192, 1024], P('seq', 'head'), may hold values from -6 to 6
- do_cells: bfloat16 [8192, 8192], P('seq', 'head'), may hold values from -6 to 6
- q_head: bfloat16 [1024, 8192], P('seq', 'head'), may hold values from -60 to 60
- k_head: bfloat16 [1024, 1024], P('seq', 'head'), may hold values from -6 to 6
- v_head: bfloat16 [1024, 1024], P('seq', 'head'), may hold values from -6 to 6
- do_head: bfloat16 [1024, 8192], P('seq', 'head'), may hold values from -6 to 6
- vis_mask: int32 [64, 8], P('seq'), may hold values from 0 to 1, as said below
Outputs:
- dq_cells: bfloat16 [8192, 8192], P('seq', 'head')
- dk_cells: bfloat16 [8192, 1024], P('seq', 'head')
- dv_cells: bfloat16 [8192, 1024], P('seq', 'head')
- dq_head: bfloat16 [1024, 8192], P('seq', 'head')
- dk_head: bfloat16 [1024, 1024], P('seq', 'head')
- dv_head: bfloat16 [1024, 1024], P('seq', 'head')
Inputs may be any that keep to these rules, and one draw needn't show every extreme that they name: vis_mask[b, t] = 1 lets the cells of block b see the headers of block t.
All inputs are finite; a program needn't handle non-finite values.
Results may differ from a plain program's by a relative error of at most 0.012.
Values may be sent and summed in bfloat16 or wider, within the bound.
A program may use at most 64 MiB of HBM per device.

v0:
```python
from functools import partial
import jax
import jax.numpy as jnp
from jax import lax
from jax.sharding import PartitionSpec as P

HD = 128
W = 256
BLOCK = 128
masked_score = -1e30


def product(pattern, former, latter):
    return jnp.einsum(pattern, former, latter, preferred_element_type=jnp.float32)


def block_stats(queries, key_rows, visible, scaling):
    scores = product("nkgd,mkd->kgnm", queries, key_rows) * scaling
    kept_scores = jnp.where(visible, scores, masked_score)
    highest = jnp.max(kept_scores, axis=-1)
    totals = jnp.sum(jnp.where(visible, jnp.exp(scores - highest[..., None]), 0.0), axis=-1)
    return (highest, totals)


def merge_stats(former, latter):
    highest = jnp.maximum(former[0], latter[0])
    return (
        highest,
        former[1] * jnp.exp(former[0] - highest) + latter[1] * jnp.exp(latter[0] - highest),
    )


def weights_of(queries, key_rows, log_totals, visible, scaling):
    scores = product("nkgd,mkd->kgnm", queries, key_rows) * scaling
    return jnp.where(visible, jnp.exp(scores - log_totals[..., None]), 0.0)


def block_delta(queries, grads_out, key_rows, value_rows, log_totals, visible, scaling):
    weights = weights_of(queries, key_rows, log_totals, visible, scaling)
    slopes = product("nkgd,mkd->kgnm", grads_out, value_rows)
    return jnp.sum(weights * slopes, axis=-1)


def block_grads(queries, grads_out, key_rows, value_rows, log_totals, deltas, visible, scaling):
    weights = weights_of(queries, key_rows, log_totals, visible, scaling)
    slopes = product("nkgd,mkd->kgnm", grads_out, value_rows)
    score_grads = weights * (slopes - deltas[..., None])
    weight_low = weights.astype(jnp.bfloat16)
    grad_low = score_grads.astype(jnp.bfloat16)
    grad_values = product("kgnm,nkgd->mkd", weight_low, grads_out)
    grad_keys = product("kgnm,nkgd->mkd", grad_low, queries) * scaling
    grad_queries = product("kgnm,mkd->nkgd", grad_low, key_rows) * scaling
    return (grad_queries, grad_keys, grad_values)


def to_rows(values):
    return jnp.transpose(values, (1, 2, 0, 3)).reshape(values.shape[1], values.shape[2], -1)


def from_rows(values, pieces):
    return jnp.transpose(values.reshape(values.shape[0], values.shape[1], pieces, -1), (2, 0, 1, 3))


def guarded(function, operands):
    return function(*operands)


def per_device(q_cells, k_cells, v_cells, do_cells, q_head, k_head, v_head, do_head, vis_mask):
    cell_count = q_cells.shape[0]
    kv_local = k_cells.shape[1] // HD
    query_local = q_cells.shape[1] // HD
    groups = query_local // kv_local
    scaling = HD ** (-0.5)
    regions = cell_count // W
    own_rows = q_head.shape[0]
    head_keys, head_values = (
        lax.all_gather(k_head, "seq", axis=0, tiled=True),
        lax.all_gather(v_head, "seq", axis=0, tiled=True),
    )
    all_queries, all_grads = (
        lax.all_gather(q_head, "seq", axis=0, tiled=True),
        lax.all_gather(do_head, "seq", axis=0, tiled=True),
    )
    header_count = head_keys.shape[0]
    blocks = header_count // BLOCK
    cell_query = q_cells.reshape(cell_count, kv_local, groups, HD)
    cell_grad = do_cells.reshape(cell_count, kv_local, groups, HD)
    cell_key = k_cells.reshape(cell_count, kv_local, HD)
    cell_value = v_cells.reshape(cell_count, kv_local, HD)
    region_query = q_cells.reshape(regions, W, kv_local, groups, HD)
    region_grad = do_cells.reshape(regions, W, kv_local, groups, HD)
    region_key = k_cells.reshape(regions, W, kv_local, HD)
    region_value = v_cells.reshape(regions, W, kv_local, HD)
    header_key_rows = head_keys.reshape(header_count, kv_local, HD)
    header_value_rows = head_values.reshape(header_count, kv_local, HD)
    key_blocks = head_keys.reshape(blocks, BLOCK, kv_local, HD)
    value_blocks = head_values.reshape(blocks, BLOCK, kv_local, HD)
    seen_blocks = jnp.transpose(jnp.repeat(vis_mask, BLOCK, axis=0) > 0)

    def outer_stat(operands):
        key_block, seen_column = operands
        return guarded(
            partial(block_stats, cell_query, scaling=scaling), (key_block, seen_column[:, None])
        )

    block_highest, block_totals = lax.map(outer_stat, (key_blocks, seen_blocks))
    outer_highest = jnp.max(block_highest, axis=0)
    outer_totals = jnp.sum(block_totals * jnp.exp(block_highest - outer_highest), axis=0)
    local_stats = jax.vmap(partial(block_stats, visible=True, scaling=scaling))(
        region_query, region_key
    )
    highest, totals = merge_stats(
        (to_rows(local_stats[0]), to_rows(local_stats[1])), (outer_highest, outer_totals)
    )
    cell_log = highest + jnp.log(totals)
    region_log = from_rows(cell_log, regions)

    def outer_delta(operands):
        key_block, value_block, seen_column = operands
        return guarded(
            partial(block_delta, cell_query, cell_grad, scaling=scaling),
            (key_block, value_block, cell_log, seen_column[:, None]),
        )

    local_delta = to_rows(
        jax.vmap(partial(block_delta, visible=True, scaling=scaling))(
            region_query, region_grad, region_key, region_value, region_log
        )
    )
    cell_delta = local_delta + jnp.sum(
        lax.map(outer_delta, (key_blocks, value_blocks, seen_blocks)), axis=0
    )
    query_zeros = jnp.zeros((cell_count, kv_local, groups, HD), jnp.float32)

    def outer_grad(running, operands):
        key_block, value_block, seen_column = operands
        gradients = guarded(
            partial(block_grads, cell_query, cell_grad, scaling=scaling),
            (key_block, value_block, cell_log, cell_delta, seen_column[:, None]),
        )
        return (running + gradients[0], (gradients[1], gradients[2]))

    outer_query, (key_parts, value_parts) = lax.scan(
        outer_grad, query_zeros, (key_blocks, value_blocks, seen_blocks)
    )
    local_grads = jax.vmap(partial(block_grads, visible=True, scaling=scaling))(
        region_query,
        region_grad,
        region_key,
        region_value,
        region_log,
        from_rows(cell_delta, regions),
    )
    query_blocks = all_queries.reshape(blocks, BLOCK, kv_local, groups, HD)
    grad_blocks = all_grads.reshape(blocks, BLOCK, kv_local, groups, HD)
    own_query = q_head.reshape(own_rows, kv_local, groups, HD)
    own_grad = do_head.reshape(own_rows, kv_local, groups, HD)
    first_row = lax.axis_index("seq") * own_rows

    def own_slice(values):
        return lax.dynamic_slice_in_dim(values, first_row, own_rows, 2)

    def own_update(values, replaced):
        return lax.dynamic_update_slice_in_dim(values, replaced, first_row, 2)

    cross_stats = lax.map(
        lambda operands: block_stats(operands, cell_key, True, scaling), query_blocks
    )
    cross_highest = to_rows(cross_stats[0])
    cross_totals = to_rows(cross_stats[1])
    self_stats = block_stats(own_query, header_key_rows, True, scaling)
    own_merged = merge_stats((own_slice(cross_highest), own_slice(cross_totals)), self_stats)
    part_highest = own_update(cross_highest, own_merged[0])
    part_totals = own_update(cross_totals, own_merged[1])
    head_highest = lax.pmax(part_highest.astype(jnp.bfloat16), "seq").astype(part_highest.dtype)
    head_totals = lax.psum(part_totals * jnp.exp(part_highest - head_highest), "seq")
    head_log = head_highest + jnp.log(head_totals)
    block_log = from_rows(head_log, blocks)
    own_log = own_slice(head_log)
    cross_delta = to_rows(
        lax.map(
            lambda operands: block_delta(
                operands[0], operands[1], cell_key, cell_value, operands[2], True, scaling
            ),
            (query_blocks, grad_blocks, block_log),
        )
    )
    self_delta = block_delta(
        own_query, own_grad, header_key_rows, header_value_rows, own_log, True, scaling
    )
    part_delta = own_update(cross_delta, own_slice(cross_delta) + self_delta)
    head_delta = lax.psum(part_delta, "seq")
    block_deltas = from_rows(head_delta, blocks)
    own_delta = own_slice(head_delta)
    key_zeros = jnp.zeros((cell_count, kv_local, HD), jnp.float32)

    def cross_grad(running, operands):
        gradients = block_grads(
            operands[0], operands[1], cell_key, cell_value, operands[2], operands[3], True, scaling
        )
        return ((running[0] + gradients[1], running[1] + gradients[2]), gradients[0])

    (cross_key, cross_value), cross_query = lax.scan(
        cross_grad, (key_zeros, key_zeros), (query_blocks, grad_blocks, block_log, block_deltas)
    )
    self_grads = block_grads(
        own_query, own_grad, header_key_rows, header_value_rows, own_log, own_delta, True, scaling
    )
    query_part = cross_query.reshape(header_count, query_local * HD)
    key_part = key_parts.reshape(header_count, kv_local * HD) + self_grads[1].reshape(
        header_count, kv_local * HD
    )
    value_part = value_parts.reshape(header_count, kv_local * HD) + self_grads[2].reshape(
        header_count, kv_local * HD
    )
    whole_sums = lax.psum((query_part, key_part, value_part), "seq")
    query_sum, key_sum, value_sum = [
        lax.dynamic_slice_in_dim(summed, first_row, own_rows, 0) for summed in whole_sums
    ]
    dq_cells = (
        local_grads[0].reshape(cell_count, query_local * HD)
        + outer_query.reshape(cell_count, query_local * HD)
    ).astype(jnp.bfloat16)
    dk_cells = (
        local_grads[1].reshape(cell_count, kv_local * HD)
        + cross_key.reshape(cell_count, kv_local * HD)
    ).astype(jnp.bfloat16)
    dv_cells = (
        local_grads[2].reshape(cell_count, kv_local * HD)
        + cross_value.reshape(cell_count, kv_local * HD)
    ).astype(jnp.bfloat16)
    dq_head = (query_sum + self_grads[0].reshape(own_rows, query_local * HD)).astype(jnp.bfloat16)
    return (
        dq_cells,
        dk_cells,
        dv_cells,
        dq_head,
        key_sum.astype(jnp.bfloat16),
        value_sum.astype(jnp.bfloat16),
    )


def solution(mesh):
    return jax.shard_map(
        per_device,
        mesh=mesh,
        in_specs=(
            P("seq", "head"),
            P("seq", "head"),
            P("seq", "head"),
            P("seq", "head"),
            P("seq", "head"),
            P("seq", "head"),
            P("seq", "head"),
            P("seq", "head"),
            P("seq", None),
        ),
        out_specs=(
            P("seq", "head"),
            P("seq", "head"),
            P("seq", "head"),
            P("seq", "head"),
            P("seq", "head"),
            P("seq", "head"),
        ),
        check_vma=False,
    )
```

profile of v0, /device:TPU:1, one launch (start us, length us, event | category | flops | bytes accessed | tf_op | source)
XLA Modules:
  0.0 988.0 jit_solution(11837171689813258582)
XLA Ops:
  9.5 47.2 %all_gather.12 = bf16[1024,128]{1,0:T(8,128)(2,1)S(1)} all-gather(bf16[32,128]{1,0:T(8,128)(2,1)} %param.26), channel_id=1, replica_groups=mesh['seq'=32,'head'=8] {'seq'}, dimensions={0}, use_global_device_ids=true | all-gather | bytes 270336 | tf_op jit(solution)/shard_map/all_gather | solution.py:77
  56.7 40.4 %all_gather.13 = bf16[1024,128]{1,0:T(8,128)(2,1)} all-gather(bf16[32,128]{1,0:T(8,128)(2,1)} %param.27), channel_id=1, replica_groups=mesh['seq'=32,'head'=8] {'seq'}, dimensions={0}, use_global_device_ids=true | all-gather | bytes 270336 | tf_op jit(solution)/shard_map/all_gather | solution.py:78
  98.7 4.6 while.74
  109.0 16.5 %while.75 = (s32[]{:T(128)}, f32[8,1,8,256]{3,2,1,0:T(8,128)}, pred[8,256]{1,0:T(8,128)(4,1)S(1)}, bf16[8,128,1,128]{3,1,2,0:T(8,128)(2,1)S(1)}, bf16[256,1,8,12...) while((s32[]{:T(128)}, f32[8,1,8,256]{3,2,1,0:T(8,128)}, ...), condition=%wide.region_11.12_spmd, body=%wide.region_9.11_spmd.sunk | while | flops 135526400 | bytes 3245173 | solution.py:131
  127.8 3.0 fusion.95
  133.0 2.2 copy.97
  137.2 37.2 %all-gather.5.cloned.1.call-done = bf16[1024,1024]{1,0:T(8,128)(2,1)} async-done(((bf16[32,1024]{1,0:T(8,128)(2,1)}), bf16[1024,1024]{1,0:T(8,128)(2,1)}) %all-gather.5.cloned.1.call-update) | async-done | bytes 2097168 | tf_op jit(solution)/shard_map/all_gather | solution.py:82
  174.4 2.2 copy.98
  179.8 18.8 %while.76 = (s32[]{:T(128)}, f32[8,1,8,128]{3,2,1,0:T(8,128)}, f32[8,1,8,128]{3,2,1,0:T(8,128)}, bf16[8,128,1,8,128]{4,1,3,2,0:T(8,128)(2,1)}, bf16[256,1,128]{2,0,1:T(8,128)(2,1)S(1)}, /*index=5*/s32[]{:T(128)}) while((s32[]{:T(128)}, f32[8,1,8,128]{3,2,1,0:T(8,128)}, f32[8,1,8,128]{3,2,1,0:T(8,128)}, ...), condition=%wide.region_18.19_spmd, body=%wide.region_15.18_spmd.sunk | while | flops 68155392 | bytes 2453589 | solution.py:166
  204.2 124.3 %pmax.7 = bf16[1,8,1024]{2,1,0:T(8,128)(2,1)} all-reduce(bf16[1,8,1024]{2,1,0:T(8,128)(2,1)} %convert_element_type.50), channel_id=1, replica_groups=mesh['seq'=32,'head'=8] {'seq'}, use_global_device_ids=true, to_apply=%region_20.21 | all-reduce | flops 8192 | bytes 32768 | tf_op jit(solution)/shard_map/pmax | solution.py:175
  329.9 128.5 %psum.35 = f32[1,8,1024]{2,1,0:T(8,128)} all-reduce(f32[1,8,1024]{2,1,0:T(8,128)} %fusion.148), channel_id=1, replica_groups=mesh['seq'=32,'head'=8] {'seq'}, use_global_device_ids=true, to_apply=%region_22.23 | all-reduce | flops 8192 | bytes 65536 | tf_op jit(solution)/shard_map/psum | solution.py:176
  460.5 31.5 %while.77 = (s32[]{:T(128)}, f32[8,1,8,128]{3,2,1,0:T(8,128)}, bf16[8,128,1,8,128]{4,1,3,2,0:T(8,128)(2,1)}, bf16[256,1,128]{2,0,1:T(8,128)(2,1)S(1)}, f32[8,1,8...) while((s32[]{:T(128)}, f32[8,1,8,128]{3,2,1,0:T(8,128)}, ...), condition=%wide.region_25.26_spmd, body=%wide.region_23.25_spmd.sunk | while | flops 135265280 | bytes 2777197 | solution.py:181
  491.9 2.6 multiply_reduce_fusion
  497.3 128.5 %psum.36 = f32[1,8,1024]{2,1,0:T(8,128)} all-reduce(f32[1,8,1024]{2,1,0:T(8,128)} %dynamic_update_slice.42), channel_id=1, replica_groups=mesh['seq'=32,'head'=8] {'seq'}, use_global_device_ids=true, to_apply=%region_27.28 | all-reduce | flops 8192 | bytes 65536 | tf_op jit(solution)/shard_map/psum | solution.py:192
  625.9 63.3 %while.79 = (s32[]{:T(128)}, f32[256,1,128]{0,2,1:T(8,128)}, f32[256,1,128]{0,2,1:T(8,128)}, f32[8,128,1,8,128]{4,3,1,0,2:T(8,128)}, bf16[8,128,1,8,128]{4,1,3,2...) while((s32[]{:T(128)}, f32[256,1,128]{0,2,1:T(8,128)}, ...), condition=%wide.region_29.30_spmd.clone, body=%wide.region_28.29_spmd.clone.sunk | while | flops 337412096 | bytes 9134296 | solution.py:203
  689.2 5.1 copy.144
  694.9 39.1 %while.78 = (s32[]{:T(128)}, f32[256,1,8,128]{0,3,2,1:T(8,128)}, f32[8,128,1,128]{3,1,2,0:T(8,128)}, f32[8,128,1,128]{3,1,2,0:T(8,128)}, bf16[8,128,1,128]{3,1,2...) while((s32[]{:T(128)}, f32[256,1,8,128]{0,3,2,1:T(8,128)}, ...), condition=%wide.region_14.15_spmd.clone, body=%wide.region_13.14_spmd.clone.sunk | while | flops 338182144 | bytes 17548512 | solution.py:143
  734.1 2.5 copy.83
  736.6 2.1 fusion.114
  740.1 2.5 copy.60
  742.7 2.6 add_convert_fusion
  749.5 140.0 %all-reduce.5 = (bf16[1024,128]{1,0:T(8,128)(2,1)S(1)}, bf16[1024,128]{1,0:T(8,128)(2,1)}) all-reduce(f32[1024,128]{1,0:T(8,128)} %fusion.104, f32[1024,128]{1,0:T(8,128)} %fusion.105), channel_id=1, replica_groups=mesh['seq'=32,'head'=8] {'seq'}, use_global_device_ids=true, to_apply=%region_31.32 | all-reduce | flops 262144 | bytes 1572864 | tf_op jit(solution)/shard_map/psum | solution.py:216
  890.8 2.4 fusion.111
  894.4 85.6 %all-reduce.4.cloned.1.call-done = f32[1024,1024]{1,0:T(8,128)} async-done(((f32[1024,1024]{1,0:T(8,128)}), f32[1024,1024]{1,0:T(8,128)}) %all-reduce.4.cloned.1.call-update) | async-done | bytes 4194320 | tf_op jit(solution)/shard_map/psum | solution.py:216
  (402 shorter events, 213.5 us)
Async XLA Ops:
  7.2 125.9 %all-gather.3.cloned.1.call-start = ((), (), s32[]{:S(2)}) async-start(), calls=%async_computation | async-start | bytes 2162688 | tf_op jit(solution)/shard_map/all_gather | solution.py:81
  7.9 166.5 %all-gather.5.cloned.1.call-start = ((), (), s32[]{:S(2)}) async-start(), calls=%async_computation.1 | async-start | bytes 2162688 | tf_op jit(solution)/shard_map/all_gather | solution.py:82
  8.6 971.3 %all-reduce.4.cloned.1.call-start = ((), (), s32[]{:S(2)}) async-start(), calls=%async_computation.2 | async-start | bytes 8388608 | tf_op jit(solution)/shard_map/psum | solution.py:216
  98.7 4.6 copy-start.9
  109.0 18.7 %copy-start.5 = (bf16[256,128]{1,0:T(8,128)(2,1)S(1)}, bf16[256,128]{1,0:T(8,128)(2,1)}, u32[]{:S(2)}) copy-start(bf16[256,128]{1,0:T(8,128)(2,1)} %param.23) | copy-start | bytes 196612
  125.5 5.2 copy-start.19
  127.8 3.0 copy-start.21
  127.8 3.0 copy-start.29
  127.8 3.0 copy-start.16
  626.6 4.5 copy-start.6
  634.5 4.5 copy-start.6
  642.4 4.5 copy-start.6
  650.3 4.5 copy-start.6
  658.2 4.5 copy-start.6
  666.1 4.5 copy-start.6
  674.1 4.5 copy-start.6
  682.0 4.5 copy-start.6
  705.1 3.0 copy-start
  724.7 3.0 copy-start
  729.6 3.0 copy-start
  740.1 6.0 copy-start.28
  742.7 3.5 copy-start.4
  742.7 3.5 copy-start.13
  749.3 143.9 %copy-start.10 = (bf16[256,1024]{1,0:T(8,128)(2,1)S(1)}, bf16[256,1024]{1,0:T(8,128)(2,1)}, u32[]{:S(2)}) copy-start(bf16[256,1024]{1,0:T(8,128)(2,1)} %param.24) | copy-start | bytes 1572868
  (39 other events, 61.4 us)
Sparse Core Ops, SparseCore 0:
  10.8 84.3 all-gather.2
  98.0 76.3 all-gather.4
  694.4 285.4 all-reduce.3
where the time goes:
time: 992 us; the launch traced here: 988 us
  blocking collectives  609 us (61%)
  matrix products  139 us (14%)
  waiting for transfers between devices  124 us (12%)
  local copies, waits for them, and re-layouts  76.3 us (8%)
  other arithmetic  23.8 us (2%)
  between operations  14.2 us (1%)
    psum x1, blocking collectives, per_device(): whole_sums = lax.psum((query_part, key_part, value_part), 'seq')  140 us
    dot_general x138, matrix products, product(): jnp.einsum(pattern, former, latter, preferred_element_type=jnp.float32)  139 us
    psum x1, blocking collectives, per_device(): head_delta = lax.psum(part_delta, 'seq')  129 us
    psum x1, blocking collectives, per_device(): lax.psum(part_totals * jnp.exp(part_highest - head_highest), 'seq')  128 us
    pmax x1, blocking collectives, per_device(): lax.pmax(part_highest.astype(jnp.bfloat16), 'seq')  124 us
    psum x1, waiting for transfers between devices, per_device(): whole_sums = lax.psum((query_part, key_part, value_part), 'seq')  85.6 us
    all_gather x1, blocking collectives, per_device(): lax.all_gather(k_head, 'seq', axis=0, tiled=True)  47.2 us
    all_gather x1, blocking collectives, per_device(): lax.all_gather(v_head, 'seq', axis=0, tiled=True)  40.4 us
  transfers between devices with their start and end apart: 3, of which 2 were waited for; matrix products, arithmetic and copies ran while one was open for 9% of the time, Pallas kernels for 0%

commit v1 on v0

--- a/solution.py
+++ b/solution.py
@@ -189,7 +189,7 @@
         own_query, own_grad, header_key_rows, header_value_rows, own_log, True, scaling
     )
     part_delta = own_update(cross_delta, own_slice(cross_delta) + self_delta)
-    head_delta = lax.psum(part_delta, "seq")
+    head_delta = lax.all_gather(part_delta, "seq").sum(axis=0)
     block_deltas = from_rows(head_delta, blocks)
     own_delta = own_slice(head_delta)
     key_zeros = jnp.zeros((cell_count, kv_local, HD), jnp.float32)

time: 992 us -> 938 us (0.946)
  blocking collectives: 609 us -> 478 us
  waiting for transfers between devices: 124 us -> 202 us
    psum x1 -> x0, blocking collectives: 129 us -> none  [per_device(): head_delta = lax.psum(part_delta, 'seq')]
    all_gather x0 -> x1, waiting for transfers between devices: none -> 59.4 us  [per_device(): head_delta = lax.all_gather(part_delta, 'seq').sum(axis=0)]
    all_gather x1, waiting for transfers between devices: 37.2 us -> 62.3 us  [per_device(): lax.all_gather(do_head, 'seq', axis=0, tiled=True)]
  transfers between devices with their start and end apart: 3 -> 4, of which waited for: 2 -> 3; matrix products, arithmetic and copies ran while one was open for 9% -> 9% of each run, Pallas kernels for 0% -> 0%
where the time goes in v1:
time: 938 us; the launch traced here: 934 us
  blocking collectives  478 us (51%)
  waiting for transfers between devices  202 us (22%)
  matrix products  139 us (15%)
  local copies, waits for them, and re-layouts  75.7 us (8%)
  other arithmetic  22.9 us (2%)
  between operations  14.2 us (2%)
    dot_general x138, matrix products, product(): jnp.einsum(pattern, former, latter, preferred_element_type=jnp.float32)  139 us
    psum x1, blocking collectives, per_device(): whole_sums = lax.psum((query_part, key_part, value_part), 'seq')  138 us
    psum x1, blocking collectives, per_device(): lax.psum(part_totals * jnp.exp(part_highest - head_highest), 'seq')  128 us
    pmax x1, blocking collectives, per_device(): lax.pmax(part_highest.astype(jnp.bfloat16), 'seq')  124 us
    psum x1, waiting for transfers between devices, per_device(): whole_sums = lax.psum((query_part, key_part, value_part), 'seq')  79.4 us
    all_gather x1, waiting for transfers between devices, per_device(): lax.all_gather(do_head, 'seq', axis=0, tiled=True)  62.3 us
    all_gather x1, waiting for transfers between devices, per_device(): head_delta = lax.all_gather(part_delta, 'seq').sum(axis=0)  59.4 us
    all_gather x1, blocking collectives, per_device(): lax.all_gather(k_head, 'seq', axis=0, tiled=True)  47.2 us
  transfers between devices with their start and end apart: 4, of which 3 were waited for; matrix products, arithmetic and copies ran while one was open for 9% of the time, Pallas kernels for 0%

profile of v1, /device:TPU:1, one launch (start us, length us, event | category | flops | bytes accessed | tf_op | source)
XLA Modules:
  0.0 934.0 jit_solution(4103294388342723394)
XLA Ops:
  9.5 47.2 %all_gather.20 = bf16[1024,128]{1,0:T(8,128)(2,1)S(1)} all-gather(bf16[32,128]{1,0:T(8,128)(2,1)} %param.26), channel_id=1, replica_groups=mesh['seq'=32,'head'=8] {'seq'}, dimensions={0}, use_global_device_ids=true | all-gather | bytes 270336 | tf_op jit(solution)/shard_map/all_gather | solution.py:77
  58.7 4.6 while.74
  63.4 40.1 %all_gather.21 = bf16[1024,128]{1,0:T(8,128)(2,1)} all-gather(bf16[32,128]{1,0:T(8,128)(2,1)S(1)} %copy-done.30), channel_id=1, replica_groups=mesh['seq'=32,'head'=8] {'seq'}, dimensions={0}, use_global_device_ids=true | all-gather | bytes 270336 | tf_op jit(solution)/shard_map/all_gather | solution.py:78
  108.1 2.2 copy.135
  112.2 62.3 %all-gather.6.cloned.1.call-done = bf16[1024,1024]{1,0:T(8,128)(2,1)} async-done(((bf16[32,1024]{1,0:T(8,128)(2,1)}), bf16[1024,1024]{1,0:T(8,128)(2,1)}) %all-gather.6.cloned.1.call-update) | async-done | bytes 2097168 | tf_op jit(solution)/shard_map/all_gather | solution.py:82
  174.5 2.2 copy.136
  179.9 18.8 %while.76 = (s32[]{:T(128)}, f32[8,1,8,128]{3,2,1,0:T(8,128)}, f32[8,1,8,128]{3,2,1,0:T(8,128)}, bf16[8,128,1,8,128]{4,1,3,2,0:T(8,128)(2,1)}, bf16[256,1,128]{2,0,1:T(8,128)(2,1)S(1)}, /*index=5*/s32[]{:T(128)}) while((s32[]{:T(128)}, f32[8,1,8,128]{3,2,1,0:T(8,128)}, f32[8,1,8,128]{3,2,1,0:T(8,128)}, ...), condition=%wide.region_18.19_spmd, body=%wide.region_15.18_spmd.sunk | while | flops 68155392 | bytes 2453589 | solution.py:166
  204.4 124.3 %pmax.7 = bf16[1,8,1024]{2,1,0:T(8,128)(2,1)} all-reduce(bf16[1,8,1024]{2,1,0:T(8,128)(2,1)} %convert_element_type.50), channel_id=1, replica_groups=mesh['seq'=32,'head'=8] {'seq'}, use_global_device_ids=true, to_apply=%region_20.21 | all-reduce | flops 8192 | bytes 32768 | tf_op jit(solution)/shard_map/pmax | solution.py:175
  330.0 128.5 %psum.28 = f32[1,8,1024]{2,1,0:T(8,128)} all-reduce(f32[1,8,1024]{2,1,0:T(8,128)} %fusion.148), channel_id=1, replica_groups=mesh['seq'=32,'head'=8] {'seq'}, use_global_device_ids=true, to_apply=%region_22.23 | all-reduce | flops 8192 | bytes 65536 | tf_op jit(solution)/shard_map/psum | solution.py:176
  460.0 31.5 %while.77 = (s32[]{:T(128)}, f32[8,1,8,128]{3,2,1,0:T(8,128)}, bf16[8,128,1,8,128]{4,1,3,2,0:T(8,128)(2,1)}, bf16[256,1,128]{2,0,1:T(8,128)(2,1)S(1)}, f32[8,1,8...) while((s32[]{:T(128)}, f32[8,1,8,128]{3,2,1,0:T(8,128)}, ...), condition=%wide.region_25.26_spmd, body=%wide.region_23.25_spmd.sunk | while | flops 135265280 | bytes 2777197 | solution.py:181
  491.5 2.6 multiply_reduce_fusion
  497.2 16.5 %while.75 = (s32[]{:T(128)}, f32[8,1,8,256]{3,2,1,0:T(8,128)}, pred[8,256]{1,0:T(8,128)(4,1)S(1)}, bf16[8,128,1,128]{3,1,2,0:T(8,128)(2,1)S(1)}, bf16[256,1,8,12...) while((s32[]{:T(128)}, f32[8,1,8,256]{3,2,1,0:T(8,128)}, ...), condition=%wide.region_11.12_spmd, body=%wide.region_9.11_spmd.sunk | while | flops 135526400 | bytes 3245173 | solution.py:131
  515.9 3.0 fusion.95
  518.9 59.4 %all-gather.8.cloned.1.call-done = f32[32,1,8,1024]{3,2,1,0:T(8,128)} async-done(((f32[1,1,8,1024]{3,2,1,0:T(8,128)}), f32[32,1,8,1024]{3,2,1,0:T(8,128)}) %all-gather.8.cloned.1.call-update) | async-done | bytes 1048592 | tf_op jit(solution)/shard_map/all_gather | solution.py:192
  580.2 63.3 %while.79 = (s32[]{:T(128)}, f32[256,1,128]{0,2,1:T(8,128)}, f32[256,1,128]{0,2,1:T(8,128)}, f32[8,128,1,8,128]{4,3,1,0,2:T(8,128)}, bf16[8,128,1,8,128]{4,1,3,2...) while((s32[]{:T(128)}, f32[256,1,128]{0,2,1:T(8,128)}, ...), condition=%wide.region_29.30_spmd.clone, body=%wide.region_28.29_spmd.clone.sunk | while | flops 337412096 | bytes 9134296 | solution.py:203
  643.5 5.1 copy.182
  649.2 39.1 %while.78 = (s32[]{:T(128)}, f32[256,1,8,128]{0,3,2,1:T(8,128)}, f32[8,128,1,128]{3,1,2,0:T(8,128)}, f32[8,128,1,128]{3,1,2,0:T(8,128)}, bf16[8,128,1,128]{3,1,2...) while((s32[]{:T(128)}, f32[256,1,8,128]{0,3,2,1:T(8,128)}, ...), condition=%wide.region_14.15_spmd.clone, body=%wide.region_13.14_spmd.clone.sunk | while | flops 338182144 | bytes 17548512 | solution.py:143
  688.4 2.5 copy.120
  690.9 2.1 fusion.114
  694.4 2.6 copy.97
  697.0 2.6 add_convert_fusion
  703.8 137.9 %all-reduce.5 = (bf16[1024,128]{1,0:T(8,128)(2,1)S(1)}, bf16[1024,128]{1,0:T(8,128)(2,1)}) all-reduce(f32[1024,128]{1,0:T(8,128)} %fusion.104, f32[1024,128]{1,0:T(8,128)} %fusion.105), channel_id=1, replica_groups=mesh['seq'=32,'head'=8] {'seq'}, use_global_device_ids=true, to_apply=%region_31.32 | all-reduce | flops 262144 | bytes 1572864 | tf_op jit(solution)/shard_map/psum | solution.py:216
  843.0 2.4 fusion.111
  846.6 79.4 %all-reduce.4.cloned.1.call-done = f32[1024,1024]{1,0:T(8,128)} async-done(((f32[1024,1024]{1,0:T(8,128)}), f32[1024,1024]{1,0:T(8,128)}) %all-reduce.4.cloned.1.call-update) | async-done | bytes 4194320 | tf_op jit(solution)/shard_map/psum | solution.py:216
  (407 shorter events, 212.2 us)
Async XLA Ops:
  7.2 51.0 %copy-start.9 = (bf16[256,1024]{1,0:T(8,128)(2,1)S(1)}, bf16[256,1024]{1,0:T(8,128)(2,1)}, u32[]{:S(2)}) copy-start(bf16[256,1024]{1,0:T(8,128)(2,1)} %param.24) | copy-start | bytes 1572868
  7.2 100.9 %all-gather.4.cloned.1.call-start = ((), (), s32[]{:S(2)}) async-start(), calls=%async_computation | async-start | bytes 2162688 | tf_op jit(solution)/shard_map/all_gather | solution.py:81
  7.9 166.6 %all-gather.6.cloned.1.call-start = ((), (), s32[]{:S(2)}) async-start(), calls=%async_computation.1 | async-start | bytes 2162688 | tf_op jit(solution)/shard_map/all_gather | solution.py:82
  8.7 569.6 %all-gather.8.cloned.1.call-start = ((), (), s32[]{:S(2)}) async-start(), calls=%async_computation.2 | async-start | bytes 1081344 | tf_op jit(solution)/shard_map/all_gather | solution.py:192
  58.7 4.7 copy-start.30
  58.7 44.8 %copy-start.15 = (bf16[32,1024]{1,0:T(8,128)(2,1)S(1)}, bf16[32,1024]{1,0:T(8,128)(2,1)}, u32[]{:S(2)}) copy-start(bf16[32,1024]{1,0:T(8,128)(2,1)} %param.25) | copy-start | bytes 196612
  63.3 42.5 %copy-start.2 = (bf16[256,128]{1,0:T(8,128)(2,1)S(1)}, bf16[256,128]{1,0:T(8,128)(2,1)}, u32[]{:S(2)}) copy-start(bf16[256,128]{1,0:T(8,128)(2,1)} %param.22) | copy-start | bytes 196612
  63.4 43.9 %copy-start.23 = (f32[8,256]{1,0:T(8,128)}, f32[8,256]{1,0:T(8,128)S(1)}, u32[]{:S(2)}) copy-start(f32[8,256]{1,0:T(8,128)S(1)} %reduce_max.52) | copy-start | bytes 24580
  63.4 44.3 %copy-start.26 = (f32[8,256]{1,0:T(8,128)}, f32[8,256]{1,0:T(8,128)S(1)}, u32[]{:S(2)}) copy-start(f32[8,256]{1,0:T(8,128)S(1)} %multiply_reduce_fusion.1) | copy-start | bytes 24580
  179.9 280.1 %copy-start.5 = (bf16[256,128]{1,0:T(8,128)(2,1)S(1)}, bf16[256,128]{1,0:T(8,128)(2,1)}, u32[]{:S(2)}) copy-start(bf16[256,128]{1,0:T(8,128)(2,1)} %param.23) | copy-start | bytes 196612
  459.4 32.1 %copy-start.27 = (f32[8,32]{1,0:T(8,128)}, f32[8,32]{1,0:T(8,128)S(1)}, u32[]{:S(2)}) copy-start(f32[8,32]{1,0:T(8,128)S(1)} %dynamic-slice_bitcast_fusion.3) | copy-start | bytes 3076
  496.3 429.7 %all-reduce.4.cloned.1.call-start = ((), (), s32[]{:S(2)}) async-start(), calls=%async_computation.3 | async-start | bytes 8388608 | tf_op jit(solution)/shard_map/psum | solution.py:216
  513.7 5.2 copy-start.18
  588.8 4.5 copy-start.6
  596.7 4.5 copy-start.6
  612.5 4.5 copy-start.6
  620.5 4.5 copy-start.6
  628.4 4.5 copy-start.6
  636.3 4.5 copy-start.6
  694.4 5.2 copy-start.4
  694.4 5.2 copy-start.14
  694.4 5.2 copy-start.28
  697.0 4.7 copy-start.13
  703.6 141.8 %copy-start.10 = (bf16[256,1024]{1,0:T(8,128)(2,1)S(1)}, bf16[256,1024]{1,0:T(8,128)(2,1)}, u32[]{:S(2)}) copy-start(bf16[256,1024]{1,0:T(8,128)(2,1)} %param.24) | copy-start | bytes 1572868
  (41 other events, 79.9 us)
Sparse Core Ops, SparseCore 0:
  10.8 84.3 all-gather.3
  98.0 76.5 all-gather.5
  496.4 81.8 all-gather.7
  648.7 277.1 all-reduce.3
